TPU v7x, 256 devices: a whole 4x4x8 slice. The times are simulated.
256 devices in a mesh: dp: 2 (over core), ctx: 128 (over z, y, x).
Axes of the slice: x: 4, y: 4, z: 8, core: 2. Of those that a mesh axis runs over, the one named last changes fastest.
Arguments:
- hidden: bfloat16 [4, 16384, 5376], P('dp', 'ctx'), parts along dimension 0, may hold values from -400 to 400
- queries: bfloat16 [4, 16384, 2048], P('dp', 'ctx'), parts along dimension 0, may hold values from -400 to 400
- input_gain: float32 [5376], replicated, may hold values from 0.1 to 1.9
- kv_weight: bfloat16 [5376, 2048], P('ctx'), may hold values from -0.078125 to 0.078125
- query_gain: float32 [128], replicated, may hold values from 1 to 2.5
- key_gain: float32 [128], replicated, may hold values from 1 to 2.5
Outputs:
- attended: bfloat16 [4, 16384, 2048], P('dp', 'ctx'), parts along dimension 0
There are 2 independent parts, one for each index of `dp`. A program takes and returns all parts, laid end to end along the dimension named above; an argument that names none is the same for every part. Nothing has to cross between parts.
All inputs are finite; a program needn't handle non-finite values.
Results may differ from a plain program's by a relative error of at most 0.012.
Values may be sent and summed in bfloat16 or wider, within the bound.
A program may use at most 128 MiB of HBM per device.

v0:
```python
import jax
import jax.numpy as jnp
from jax import lax
from jax.sharding import PartitionSpec as P

HD = 128
WINDOW = 1024
attn_scalar = 168.0
norm_eps = 1e-06


def from_behind(block, axis, distance):
    devices = range(lax.axis_size(axis))
    route = [(i - distance, i) for i in devices if i - distance in devices]
    return lax.ppermute(block, axis, route)


def rotary_tables(positions, head_width):
    half_width = head_width // 2
    exponent = 2.0 * jnp.arange(half_width, dtype=jnp.float32) / head_width
    inverse = jnp.power(10000.0, -exponent)
    angles = positions.astype(jnp.float32)[:, None] * inverse[None, :]
    return (jnp.cos(angles), jnp.sin(angles))


def rotate(heads, cos_table, sine_table):
    half_width = heads.shape[-1] // 2
    first = heads[..., :half_width]
    second = heads[..., half_width:]
    cos_part = cos_table[:, None, :]
    sine_part = sine_table[:, None, :]
    return jnp.concatenate(
        [first * cos_part - second * sine_part, second * cos_part + first * sine_part], axis=-1
    )


def head_norm(heads, gain):
    return heads * lax.rsqrt(jnp.mean(heads * heads, axis=-1, keepdims=True) + norm_eps) * gain


def body(hidden, queries, input_gain, kv_weight, query_gain, key_gain):
    seq_count, block_len, model_width = hidden.shape
    kv_width = kv_weight.shape[1]
    kv_half = kv_width // 2
    kv_heads = kv_half // HD
    query_heads = queries.shape[2] // HD
    group_size = query_heads // kv_heads
    span_blocks = WINDOW // block_len
    token_rows = seq_count * block_len
    hidden_f32 = hidden.astype(jnp.float32)
    normed = (
        hidden_f32
        * lax.rsqrt(jnp.mean(hidden_f32 * hidden_f32, axis=-1, keepdims=True) + norm_eps)
        * input_gain
    )
    normed = normed.astype(jnp.bfloat16).reshape(token_rows, model_width)
    projected = jnp.dot(
        normed,
        lax.all_gather(kv_weight, "ctx", axis=0, tiled=True),
        preferred_element_type=jnp.float32,
    )
    key_proj = projected[:, :kv_half]
    value_proj = projected[:, kv_half:]
    shard_index = lax.axis_index("ctx")
    positions = shard_index * block_len + jnp.arange(block_len, dtype=jnp.int32)
    cos_table, sine_table = rotary_tables(positions, HD)
    key_part = key_proj.reshape(seq_count, block_len, kv_heads, HD)
    key_part = rotate(head_norm(key_part, key_gain), cos_table, sine_table).astype(jnp.bfloat16)
    value_part = value_proj.reshape(seq_count, block_len, kv_half).astype(jnp.bfloat16)
    key_block = jnp.concatenate(
        [key_part.reshape(seq_count, block_len, kv_half), value_part], axis=2
    )
    query_part = queries.astype(jnp.float32).reshape(seq_count, block_len, query_heads, HD)
    query_part = (
        rotate(head_norm(query_part, query_gain), cos_table, sine_table) * attn_scalar ** (-0.5)
    ).astype(jnp.bfloat16)
    previous = from_behind(key_block, "ctx", 1)
    pieces = [previous]
    for offset in range(2, span_blocks + 1):
        pieces.append(from_behind(key_block, "ctx", offset))
    window_blocks = jnp.concatenate(pieces[::-1] + [key_block], axis=1)
    key_pos = (shard_index - span_blocks) * block_len + jnp.arange(
        (span_blocks + 1) * block_len, dtype=jnp.int32
    )
    allowed = (
        (key_pos[None, :] <= positions[:, None])
        & (key_pos[None, :] > positions[:, None] - WINDOW)
        & (key_pos[None, :] >= 0)
    )
    outputs = []
    for seq_index in range(seq_count):
        window_keys = window_blocks[seq_index, :, :kv_half].reshape(-1, kv_heads, HD)
        window_values = window_blocks[seq_index, :, kv_half:].reshape(-1, kv_heads, HD)
        query_block = query_part[seq_index].reshape(block_len, kv_heads, group_size, HD)
        scores = jnp.einsum(
            "qhgd,khd->hgqk", query_block, window_keys, preferred_element_type=jnp.float32
        )
        weights = jnp.where(allowed, jnp.exp(scores), 0.0)
        row_total = jnp.sum(weights, axis=-1)
        weighted = jnp.einsum(
            "hgqk,khd->qhgd",
            weights.astype(jnp.bfloat16),
            window_values,
            preferred_element_type=jnp.float32,
        )
        result = weighted / jnp.transpose(row_total, (2, 0, 1))[..., None]
        outputs.append(result.astype(jnp.bfloat16).reshape(block_len, query_heads * HD))
    return jnp.stack(outputs, axis=0)


def solution(mesh):
    return jax.shard_map(
        body,
        mesh=mesh,
        in_specs=(P("dp", "ctx", None), P("dp", "ctx", None), P(), P("ctx", None), P(), P()),
        out_specs=P("dp", "ctx", None),
        check_vma=False,
    )
```

profile of v0, /device:TPU:64, one launch (start us, length us, event | category | flops | bytes accessed | tf_op | source)
XLA Modules:
  0.0 528.8 jit_solution(4616291720321876393)
XLA Ops:
  7.3 1.5 copy.71
  9.7 2.6 fusion.4
  13.4 2.2 fusion.6
  15.7 174.9 %all-gather.3.cloned.1.call-done = bf16[128,42,2048]{2,1,0:T(8,128)(2,1)} async-done(((bf16[1,42,2048]{2,1,0:T(8,128)(2,1)}), bf16[128,42,2048]{2,1,0:T(8,128)(2,1)}) %all-gather.3.cloned.1.call-update) | async-done | bytes 22020112 | tf_op jit(solution)/shard_map/all_gather | solution.py:59
  190.5 27.7 %reshape.131 = bf16[5376,2048]{1,0:T(8,128)(2,1)} reshape(bf16[128,42,2048]{2,1,0:T(8,128)(2,1)} %all-gather.3.cloned.1.call-done) | data formatting | bytes 44040192
  218.2 11.1 %fusion.35 = f32[256,2048]{1,0:T(8,128)S(1)} fusion(bf16[256,5376]{1,0:T(8,128)(2,1)} %bitcast.101, bf16[5376,2048]{1,0:T(8,128)(2,1)} %reshape.131), kind=kOutput, calls=%fused_computation.65 | convolution fusion | flops 5637144576 | bytes 26869760 | tf_op jit(solution)/shard_map/dot_general | solution.py:57
  231.4 1.6 copy.46
  233.0 1.3 add_rsqrt_fusion.1
  234.3 1.5 copy.47
  235.8 1.3 fusion.25
  238.2 1.3 copy.49
  239.6 4.9 collective-permute-start
  244.5 2.8 collective-permute-start.1
  247.3 1.4 fusion.16
  248.6 6.4 %collective-permute-start.2 = (bf16[2,128,2048]{1,2,0:T(8,128)(2,1)S(1)}, bf16[2,128,2048]{1,2,0:T(8,128)(2,1)S(1)}, u32[]{:S(2)}, u32[]{:S(2)}) collective-permute-start(bf16[2,128,2048]{1,2,0:T(8,128)(2,1)S(1)} %pad_maximum_fusion), channel_id=1, source_target_pairs={{0,6},{1,7},{2,8},{3,9},{4,10},{5,11},{6,12},{7,13},{8,14},{9,15},... | collective-permute-start | bytes 3145736 | tf_op jit(solution)/shard_map/ppermute | solution.py:15
  255.7 3.4 collective-permute-start.3
  259.7 3.1 collective-permute-start.4
  263.3 72.2 %collective-permute-done = bf16[2,128,2048]{1,2,0:T(8,128)(2,1)S(1)} collective-permute-done((bf16[2,128,2048]{1,2,0:T(8,128)(2,1)S(1)}, bf16[2,128,2048]{1,2,0:T(8,128)(2,1)S(1)}, u32[]{:S(2)}, u32[]{:S(2)}) %collective-permute-start) | collective-permute-done | bytes 1048608 | tf_op jit(solution)/shard_map/ppermute | solution.py:15
  335.5 5.4 %collective-permute-start.5 = (bf16[2,128,2048]{1,2,0:T(8,128)(2,1)S(1)}, bf16[2,128,2048]{1,2,0:T(8,128)(2,1)S(1)}, u32[]{:S(2)}, u32[]{:S(2)}) collective-permute-start(bf16[2,128,2048]{1,2,0:T(8,128)(2,1)S(1)} %pad_maximum_fusion), channel_id=1, source_target_pairs={{0,3},{1,4},{2,5},{3,6},{4,7},{5,8},{6,9},{7,10},{8,11},{9,12},{10... | collective-permute-start | bytes 3145736 | tf_op jit(solution)/shard_map/ppermute | solution.py:15
  341.1 23.2 %collective-permute-start.6 = (bf16[2,128,2048]{1,2,0:T(8,128)(2,1)S(1)}, bf16[2,128,2048]{1,2,0:T(8,128)(2,1)S(1)}, u32[]{:S(2)}, u32[]{:S(2)}) collective-permute-start(bf16[2,128,2048]{1,2,0:T(8,128)(2,1)S(1)} %pad_maximum_fusion), channel_id=1, source_target_pairs={{0,2},{1,3},{2,4},{3,5},{4,6},{5,7},{6,8},{7,9},{8,10},{9,11},{10,... | collective-permute-start | bytes 3145736 | tf_op jit(solution)/shard_map/ppermute | solution.py:15
  364.6 34.9 %collective-permute-start.7 = (bf16[2,128,2048]{1,2,0:T(8,128)(2,1)S(1)}, bf16[2,128,2048]{1,2,0:T(8,128)(2,1)S(1)}, u32[]{:S(2)}, u32[]{:S(2)}) collective-permute-start(bf16[2,128,2048]{1,2,0:T(8,128)(2,1)S(1)} %pad_maximum_fusion), channel_id=1, source_target_pairs={{0,1},{1,2},{2,3},{3,4},{4,5},{5,6},{6,7},{7,8},{8,9},{9,10},{10,1... | collective-permute-start | bytes 3145736 | tf_op jit(solution)/shard_map/ppermute | solution.py:15
  399.7 32.0 %collective-permute-done.3 = bf16[2,128,2048]{1,2,0:T(8,128)(2,1)S(1)} collective-permute-done((bf16[2,128,2048]{1,2,0:T(8,128)(2,1)S(1)}, bf16[2,128,2048]{1,2,0:T(8,128)(2,1)S(1)}, u32[]{:S(2)}, u32[]{:S(2)}) %collective-permute-start.3) | collective-permute-done | bytes 1048608 | tf_op jit(solution)/shard_map/ppermute | solution.py:15
  432.0 8.6 %collective-permute-done.4 = bf16[2,128,2048]{1,2,0:T(8,128)(2,1)S(1)} collective-permute-done((bf16[2,128,2048]{1,2,0:T(8,128)(2,1)S(1)}, bf16[2,128,2048]{1,2,0:T(8,128)(2,1)S(1)}, u32[]{:S(2)}, u32[]{:S(2)}) %collective-permute-start.4) | collective-permute-done | bytes 1048608 | tf_op jit(solution)/shard_map/ppermute | solution.py:15
  440.9 13.0 %collective-permute-done.5 = bf16[2,128,2048]{1,2,0:T(8,128)(2,1)S(1)} collective-permute-done((bf16[2,128,2048]{1,2,0:T(8,128)(2,1)S(1)}, bf16[2,128,2048]{1,2,0:T(8,128)(2,1)S(1)}, u32[]{:S(2)}, u32[]{:S(2)}) %collective-permute-start.5) | collective-permute-done | bytes 1048608 | tf_op jit(solution)/shard_map/ppermute | solution.py:15
  454.1 44.2 %collective-permute-done.6 = bf16[2,128,2048]{1,2,0:T(8,128)(2,1)S(1)} collective-permute-done((bf16[2,128,2048]{1,2,0:T(8,128)(2,1)S(1)}, bf16[2,128,2048]{1,2,0:T(8,128)(2,1)S(1)}, u32[]{:S(2)}, u32[]{:S(2)}) %collective-permute-start.6) | collective-permute-done | bytes 1048608 | tf_op jit(solution)/shard_map/ppermute | solution.py:15
  498.5 1.8 collective-permute-done.7
  500.8 2.0 fusion.33
  502.9 1.4 fusion.36
  504.3 3.6 fusion
  508.0 4.2 divide_convert_fusion.1
  513.4 6.2 %divide_convert_fusion = bf16[128,8,2,128]{0,3,2,1:T(8,128)(2,1)} fusion(bf16[1152,8,128,1]{0,2,3,1:T(8,128)(2,1)S(1)} %bitcast.102, f32[8,1152,128,2]{2,1,3,0:T(8,128)} %copy-done, pred[128,1152]{0,1:T(8,128)(4,1)S(1)} %and_and_fusion, f32[128,8,2]{0,2,1:T(2,128)S(1)} %bitcast.111), kind=kOutput, calls=%fused_computation.35 | convolution fusion | flops 609222656 | bytes 12476416 | tf_op jit(solution)/shard_map/hgqk,khd->qhgd/dot_general | solution.py:100
  519.7 1.2 copy.59
  (46 shorter events, 12.2 us)
Async XLA Ops:
  6.5 184.0 %all-gather.3.cloned.1.call-start = ((), (), s32[]{:S(2)}) async-start(), calls=%async_computation | async-start | bytes 25362432 | tf_op jit(solution)/shard_map/all_gather | solution.py:59
  8.7 4.7 copy-start.2
  9.6 3.9 copy-start.1
  239.6 96.0 %collective-permute-start = (bf16[2,128,2048]{1,2,0:T(8,128)(2,1)S(1)}, bf16[2,128,2048]{1,2,0:T(8,128)(2,1)S(1)}, u32[]{:S(2)}, u32[]{:S(2)}) collective-permute-start(bf16[2,128,2048]{1,2,0:T(8,128)(2,1)S(1)} %pad_maximum_fusion), channel_id=1, source_target_pairs={{0,8},{1,9},{2,10},{3,11},{4,12},{5,13},{6,14},{7,15},{8,16},{9,17... | collective-permute-start | bytes 3145736 | tf_op jit(solution)/shard_map/ppermute | solution.py:15
  244.5 96.6 %collective-permute-start.1 = (bf16[2,128,2048]{1,2,0:T(8,128)(2,1)S(1)}, bf16[2,128,2048]{1,2,0:T(8,128)(2,1)S(1)}, u32[]{:S(2)}, u32[]{:S(2)}) collective-permute-start(bf16[2,128,2048]{1,2,0:T(8,128)(2,1)S(1)} %pad_maximum_fusion), channel_id=1, source_target_pairs={{0,7},{1,8},{2,9},{3,10},{4,11},{5,12},{6,13},{7,14},{8,15},{9,16}... | collective-permute-start | bytes 3145736 | tf_op jit(solution)/shard_map/ppermute | solution.py:15
  248.6 115.9 %collective-permute-start.2 = (bf16[2,128,2048]{1,2,0:T(8,128)(2,1)S(1)}, bf16[2,128,2048]{1,2,0:T(8,128)(2,1)S(1)}, u32[]{:S(2)}, u32[]{:S(2)}) collective-permute-start(bf16[2,128,2048]{1,2,0:T(8,128)(2,1)S(1)} %pad_maximum_fusion), channel_id=1, source_target_pairs={{0,6},{1,7},{2,8},{3,9},{4,10},{5,11},{6,12},{7,13},{8,14},{9,15},... | collective-permute-start | bytes 3145736 | tf_op jit(solution)/shard_map/ppermute | solution.py:15
  255.7 176.1 %collective-permute-start.3 = (bf16[2,128,2048]{1,2,0:T(8,128)(2,1)S(1)}, bf16[2,128,2048]{1,2,0:T(8,128)(2,1)S(1)}, u32[]{:S(2)}, u32[]{:S(2)}) collective-permute-start(bf16[2,128,2048]{1,2,0:T(8,128)(2,1)S(1)} %pad_maximum_fusion), channel_id=1, source_target_pairs={{0,5},{1,6},{2,7},{3,8},{4,9},{5,10},{6,11},{7,12},{8,13},{9,14},{... | collective-permute-start | bytes 3145736 | tf_op jit(solution)/shard_map/ppermute | solution.py:15
  259.7 180.9 %collective-permute-start.4 = (bf16[2,128,2048]{1,2,0:T(8,128)(2,1)S(1)}, bf16[2,128,2048]{1,2,0:T(8,128)(2,1)S(1)}, u32[]{:S(2)}, u32[]{:S(2)}) collective-permute-start(bf16[2,128,2048]{1,2,0:T(8,128)(2,1)S(1)} %pad_maximum_fusion), channel_id=1, source_target_pairs={{0,4},{1,5},{2,6},{3,7},{4,8},{5,9},{6,10},{7,11},{8,12},{9,13},{1... | collective-permute-start | bytes 3145736 | tf_op jit(solution)/shard_map/ppermute | solution.py:15
  335.5 118.3 %collective-permute-start.5 = (bf16[2,128,2048]{1,2,0:T(8,128)(2,1)S(1)}, bf16[2,128,2048]{1,2,0:T(8,128)(2,1)S(1)}, u32[]{:S(2)}, u32[]{:S(2)}) collective-permute-start(bf16[2,128,2048]{1,2,0:T(8,128)(2,1)S(1)} %pad_maximum_fusion), channel_id=1, source_target_pairs={{0,3},{1,4},{2,5},{3,6},{4,7},{5,8},{6,9},{7,10},{8,11},{9,12},{10... | collective-permute-start | bytes 3145736 | tf_op jit(solution)/shard_map/ppermute | solution.py:15
  341.1 157.2 %collective-permute-start.6 = (bf16[2,128,2048]{1,2,0:T(8,128)(2,1)S(1)}, bf16[2,128,2048]{1,2,0:T(8,128)(2,1)S(1)}, u32[]{:S(2)}, u32[]{:S(2)}) collective-permute-start(bf16[2,128,2048]{1,2,0:T(8,128)(2,1)S(1)} %pad_maximum_fusion), channel_id=1, source_target_pairs={{0,2},{1,3},{2,4},{3,5},{4,6},{5,7},{6,8},{7,9},{8,10},{9,11},{10,... | collective-permute-start | bytes 3145736 | tf_op jit(solution)/shard_map/ppermute | solution.py:15
  364.6 135.7 %collective-permute-start.7 = (bf16[2,128,2048]{1,2,0:T(8,128)(2,1)S(1)}, bf16[2,128,2048]{1,2,0:T(8,128)(2,1)S(1)}, u32[]{:S(2)}, u32[]{:S(2)}) collective-permute-start(bf16[2,128,2048]{1,2,0:T(8,128)(2,1)S(1)} %pad_maximum_fusion), channel_id=1, source_target_pairs={{0,1},{1,2},{2,3},{3,4},{4,5},{5,6},{6,7},{7,8},{8,9},{9,10},{10,1... | collective-permute-start | bytes 3145736 | tf_op jit(solution)/shard_map/ppermute | solution.py:15
  504.3 3.7 copy-start
Sparse Core Ops, SparseCore 0:
  11.0 179.4 all-gather.2
where the time goes:
time: 530 us; the launch traced here: 529 us
  waiting for transfers between devices  347 us (65%)
  starting transfers between devices  84 us (16%)
  local copies, waits for them, and re-layouts  42.1 us (8%)
  matrix products  26.6 us (5%)
  other arithmetic  14.9 us (3%)
  between operations  13.8 us (3%)
    all_gather x1, waiting for transfers between devices, body(): lax.all_gather(kv_weight, 'ctx', axis=0, tiled=True)  175 us
    ppermute x8, waiting for transfers between devices, from_behind(): return lax.ppermute(block, axis, route)  172 us
    ppermute x8, starting transfers between devices, from_behind(): return lax.ppermute(block, axis, route)  84 us
    unnamed x18, local copies, waits for them, and re-layouts  31.4 us
    dot_general x1, matrix products, body(): jnp.dot(normed, lax.all_gather(kv_weight, 'ctx', axis=0, tiled=True), pre...  11.1 us
  transfers between devices with their start and end apart: 9, of which 7 were waited for; matrix products, arithmetic and copies ran while one was open for 2% of the time, Pallas kernels for 0%

commit v1 on v0

--- a/solution.py
+++ b/solution.py
@@ -54,11 +54,14 @@
         * input_gain
     )
     normed = normed.astype(jnp.bfloat16).reshape(token_rows, model_width)
-    projected = jnp.dot(
-        normed,
-        lax.all_gather(kv_weight, "ctx", axis=0, tiled=True),
-        preferred_element_type=jnp.float32,
-    )
+
+    def _note_threads(raw):
+        runs = []
+        for _ in range(lax.axis_size("ctx")):
+            runs.append(raw)
+        return jnp.concatenate(lax.all_to_all(jnp.stack(runs, 0), "ctx", 0, 0), 0)
+
+    projected = jnp.dot(normed, _note_threads(kv_weight), preferred_element_type=jnp.float32)
     key_proj = projected[:, :kv_half]
     value_proj = projected[:, kv_half:]
     shard_index = lax.axis_index("ctx")

time: 530 us -> 931 us (1.76)
  the two profiles are of different devices: /device:TPU:64 before, /device:TPU:160 now
where the time goes in v1:
time: 931 us; the launch traced here: 930 us
  waiting for transfers between devices  748 us (80%)
  starting transfers between devices  89 us (10%)
  local copies, waits for them, and re-layouts  50.3 us (5%)
  matrix products  26.6 us (3%)
  other arithmetic  14.9 us (2%)
    all_to_all x1, waiting for transfers between devices, _note_threads(): return jnp.concatenate(lax.all_to_all(jnp.stack(runs, 0), 'ctx', 0, 0), 0)  557 us
    ppermute x8, waiting for transfers between devices, from_behind(): return lax.ppermute(block, axis, route)  191 us
    ppermute x8, starting transfers between devices, from_behind(): return lax.ppermute(block, axis, route)  74.8 us
    reshape x1, local copies, waits for them, and re-layouts, _note_threads(): return jnp.concatenate(lax.all_to_all(jnp.stack(runs, 0), 'ctx', 0, 0), 0)  27.7 us
  transfers between devices with their start and end apart: 9, of which 7 were waited for; matrix products, arithmetic and copies ran while one was open for 1% of the time, Pallas kernels for 0%

profile of v1, /device:TPU:160, one launch (start us, length us, event | category | flops | bytes accessed | tf_op | source)
XLA Modules:
  0.0 929.5 jit_solution(9349696965694032198)
XLA Ops:
  0.0 9.3 %stack.4 = bf16[128,42,2048]{2,1,0:T(8,128)(2,1)} broadcast(bf16[42,2048]{1,0:T(8,128)(2,1)} %param.9), dimensions={1,2} | broadcast | bytes 22192128 | tf_op jit(solution)/shard_map/stack | solution.py:62
  9.3 14.1 %all-to-all-start = ((bf16[128,42,2048]{2,1,0:T(8,128)(2,1)}), bf16[128,42,2048]{2,1,0:T(8,128)(2,1)}, u32[]{:S(2)}, u32[]{:S(2)}) async-start(bf16[128,42,2048]{2,1,0:T(8,128)(2,1)} %stack.4), calls=%async_computation | async-start | bytes 50331648 | tf_op jit(solution)/shard_map/all_to_all | solution.py:62
  24.7 2.6 fusion.4
  28.5 2.2 fusion.6
  30.7 557.4 %all-to-all-done = bf16[128,42,2048]{2,1,0:T(8,128)(2,1)} async-done(((bf16[128,42,2048]{2,1,0:T(8,128)(2,1)}), bf16[128,42,2048]{2,1,0:T(8,128)(2,1)}, u32[]{:S(2)}, u32[]{:S(2)}) %all-to-all-start) | async-done | bytes 22020128 | tf_op jit(solution)/shard_map/all_to_all | solution.py:62
  588.1 27.7 %reshape.130 = bf16[5376,2048]{1,0:T(8,128)(2,1)} reshape(bf16[128,42,2048]{2,1,0:T(8,128)(2,1)} %all-to-all-done) | data formatting | bytes 44040192 | tf_op jit(solution)/shard_map/reshape | solution.py:62
  615.8 11.1 %fusion.35 = f32[256,2048]{1,0:T(8,128)S(1)} fusion(bf16[256,5376]{1,0:T(8,128)(2,1)} %bitcast.100, bf16[5376,2048]{1,0:T(8,128)(2,1)} %reshape.130), kind=kOutput, calls=%fused_computation.65 | convolution fusion | flops 5637144576 | bytes 26869760 | tf_op jit(solution)/shard_map/dot_general | solution.py:64
  629.0 1.6 copy.46
  630.6 1.3 add_rsqrt_fusion.1
  631.8 1.5 copy.47
  633.3 1.3 fusion.25
  635.7 1.3 copy.49
  637.1 9.0 collective-permute-start
  646.1 1.9 collective-permute-start.1
  648.0 1.4 fusion.16
  649.4 1.9 collective-permute-start.2
  652.0 3.4 collective-permute-start.3
  656.0 11.1 %collective-permute-start.4 = (bf16[2,128,2048]{1,2,0:T(8,128)(2,1)S(1)}, bf16[2,128,2048]{1,2,0:T(8,128)(2,1)S(1)}, u32[]{:S(2)}, u32[]{:S(2)}) collective-permute-start(bf16[2,128,2048]{1,2,0:T(8,128)(2,1)S(1)} %pad_maximum_fusion), channel_id=1, source_target_pairs={{0,4},{1,5},{2,6},{3,7},{4,8},{5,9},{6,10},{7,11},{8,12},{9,13},{1... | collective-permute-start | bytes 3145736 | tf_op jit(solution)/shard_map/ppermute | solution.py:15
  667.7 69.5 %collective-permute-done = bf16[2,128,2048]{1,2,0:T(8,128)(2,1)S(1)} collective-permute-done((bf16[2,128,2048]{1,2,0:T(8,128)(2,1)S(1)}, bf16[2,128,2048]{1,2,0:T(8,128)(2,1)S(1)}, u32[]{:S(2)}, u32[]{:S(2)}) %collective-permute-start) | collective-permute-done | bytes 1048608 | tf_op jit(solution)/shard_map/ppermute | solution.py:15
  737.2 2.9 collective-permute-start.5
  740.2 20.3 %collective-permute-start.6 = (bf16[2,128,2048]{1,2,0:T(8,128)(2,1)S(1)}, bf16[2,128,2048]{1,2,0:T(8,128)(2,1)S(1)}, u32[]{:S(2)}, u32[]{:S(2)}) collective-permute-start(bf16[2,128,2048]{1,2,0:T(8,128)(2,1)S(1)} %pad_maximum_fusion), channel_id=1, source_target_pairs={{0,2},{1,3},{2,4},{3,5},{4,6},{5,7},{6,8},{7,9},{8,10},{9,11},{10,... | collective-permute-start | bytes 3145736 | tf_op jit(solution)/shard_map/ppermute | solution.py:15
  760.8 24.3 %collective-permute-start.7 = (bf16[2,128,2048]{1,2,0:T(8,128)(2,1)S(1)}, bf16[2,128,2048]{1,2,0:T(8,128)(2,1)S(1)}, u32[]{:S(2)}, u32[]{:S(2)}) collective-permute-start(bf16[2,128,2048]{1,2,0:T(8,128)(2,1)S(1)} %pad_maximum_fusion), channel_id=1, source_target_pairs={{0,1},{1,2},{2,3},{3,4},{4,5},{5,6},{6,7},{7,8},{8,9},{9,10},{10,1... | collective-permute-start | bytes 3145736 | tf_op jit(solution)/shard_map/ppermute | solution.py:15
  785.3 36.8 %collective-permute-done.3 = bf16[2,128,2048]{1,2,0:T(8,128)(2,1)S(1)} collective-permute-done((bf16[2,128,2048]{1,2,0:T(8,128)(2,1)S(1)}, bf16[2,128,2048]{1,2,0:T(8,128)(2,1)S(1)}, u32[]{:S(2)}, u32[]{:S(2)}) %collective-permute-start.3) | collective-permute-done | bytes 1048608 | tf_op jit(solution)/shard_map/ppermute | solution.py:15
  822.4 28.2 %collective-permute-done.4 = bf16[2,128,2048]{1,2,0:T(8,128)(2,1)S(1)} collective-permute-done((bf16[2,128,2048]{1,2,0:T(8,128)(2,1)S(1)}, bf16[2,128,2048]{1,2,0:T(8,128)(2,1)S(1)}, u32[]{:S(2)}, u32[]{:S(2)}) %collective-permute-start.4) | collective-permute-done | bytes 1048608 | tf_op jit(solution)/shard_map/ppermute | solution.py:15
  850.9 5.7 collective-permute-done.5
  856.8 45.3 %collective-permute-done.6 = bf16[2,128,2048]{1,2,0:T(8,128)(2,1)S(1)} collective-permute-done((bf16[2,128,2048]{1,2,0:T(8,128)(2,1)S(1)}, bf16[2,128,2048]{1,2,0:T(8,128)(2,1)S(1)}, u32[]{:S(2)}, u32[]{:S(2)}) %collective-permute-start.6) | collective-permute-done | bytes 1048608 | tf_op jit(solution)/shard_map/ppermute | solution.py:15
  902.4 5.5 collective-permute-done.7
  908.4 2.0 fusion.33
  910.4 1.4 fusion.36
  911.9 3.6 fusion
  915.5 4.2 divide_convert_fusion.1
  921.0 6.2 divide_convert_fusion
  (48 shorter events, 13.0 us)
Async XLA Ops:
  9.3 14.2 %copy-start.2 = (bf16[2,128,2048]{2,1,0:T(8,128)(2,1)S(1)}, bf16[2,128,2048]{2,1,0:T(8,128)(2,1)}, u32[]{:S(2)}) copy-start(bf16[2,128,2048]{2,1,0:T(8,128)(2,1)} %param.7) | copy-start | bytes 3145732
  9.3 578.7 %all-to-all-start = ((bf16[128,42,2048]{2,1,0:T(8,128)(2,1)}), bf16[128,42,2048]{2,1,0:T(8,128)(2,1)}, u32[]{:S(2)}, u32[]{:S(2)}) async-start(bf16[128,42,2048]{2,1,0:T(8,128)(2,1)} %stack.4), calls=%async_computation | async-start | bytes 50331648 | tf_op jit(solution)/shard_map/all_to_all | solution.py:62
  23.8 4.7 copy-start.3
  24.6 3.9 copy-start.1
  637.1 100.0 %collective-permute-start = (bf16[2,128,2048]{1,2,0:T(8,128)(2,1)S(1)}, bf16[2,128,2048]{1,2,0:T(8,128)(2,1)S(1)}, u32[]{:S(2)}, u32[]{:S(2)}) collective-permute-start(bf16[2,128,2048]{1,2,0:T(8,128)(2,1)S(1)} %pad_maximum_fusion), channel_id=1, source_target_pairs={{0,8},{1,9},{2,10},{3,11},{4,12},{5,13},{6,14},{7,15},{8,16},{9,17... | collective-permute-start | bytes 3145736 | tf_op jit(solution)/shard_map/ppermute | solution.py:15
  646.1 94.1 %collective-permute-start.1 = (bf16[2,128,2048]{1,2,0:T(8,128)(2,1)S(1)}, bf16[2,128,2048]{1,2,0:T(8,128)(2,1)S(1)}, u32[]{:S(2)}, u32[]{:S(2)}) collective-permute-start(bf16[2,128,2048]{1,2,0:T(8,128)(2,1)S(1)} %pad_maximum_fusion), channel_id=1, source_target_pairs={{0,7},{1,8},{2,9},{3,10},{4,11},{5,12},{6,13},{7,14},{8,15},{9,16}... | collective-permute-start | bytes 3145736 | tf_op jit(solution)/shard_map/ppermute | solution.py:15
  649.4 111.4 %collective-permute-start.2 = (bf16[2,128,2048]{1,2,0:T(8,128)(2,1)S(1)}, bf16[2,128,2048]{1,2,0:T(8,128)(2,1)S(1)}, u32[]{:S(2)}, u32[]{:S(2)}) collective-permute-start(bf16[2,128,2048]{1,2,0:T(8,128)(2,1)S(1)} %pad_maximum_fusion), channel_id=1, source_target_pairs={{0,6},{1,7},{2,8},{3,9},{4,10},{5,11},{6,12},{7,13},{8,14},{9,15},... | collective-permute-start | bytes 3145736 | tf_op jit(solution)/shard_map/ppermute | solution.py:15
  652.0 170.2 %collective-permute-start.3 = (bf16[2,128,2048]{1,2,0:T(8,128)(2,1)S(1)}, bf16[2,128,2048]{1,2,0:T(8,128)(2,1)S(1)}, u32[]{:S(2)}, u32[]{:S(2)}) collective-permute-start(bf16[2,128,2048]{1,2,0:T(8,128)(2,1)S(1)} %pad_maximum_fusion), channel_id=1, source_target_pairs={{0,5},{1,6},{2,7},{3,8},{4,9},{5,10},{6,11},{7,12},{8,13},{9,14},{... | collective-permute-start | bytes 3145736 | tf_op jit(solution)/shard_map/ppermute | solution.py:15
  656.0 194.6 %collective-permute-start.4 = (bf16[2,128,2048]{1,2,0:T(8,128)(2,1)S(1)}, bf16[2,128,2048]{1,2,0:T(8,128)(2,1)S(1)}, u32[]{:S(2)}, u32[]{:S(2)}) collective-permute-start(bf16[2,128,2048]{1,2,0:T(8,128)(2,1)S(1)} %pad_maximum_fusion), channel_id=1, source_target_pairs={{0,4},{1,5},{2,6},{3,7},{4,8},{5,9},{6,10},{7,11},{8,12},{9,13},{1... | collective-permute-start | bytes 3145736 | tf_op jit(solution)/shard_map/ppermute | solution.py:15
  737.2 119.4 %collective-permute-start.5 = (bf16[2,128,2048]{1,2,0:T(8,128)(2,1)S(1)}, bf16[2,128,2048]{1,2,0:T(8,128)(2,1)S(1)}, u32[]{:S(2)}, u32[]{:S(2)}) collective-permute-start(bf16[2,128,2048]{1,2,0:T(8,128)(2,1)S(1)} %pad_maximum_fusion), channel_id=1, source_target_pairs={{0,3},{1,4},{2,5},{3,6},{4,7},{5,8},{6,9},{7,10},{8,11},{9,12},{10... | collective-permute-start | bytes 3145736 | tf_op jit(solution)/shard_map/ppermute | solution.py:15
  740.2 161.9 %collective-permute-start.6 = (bf16[2,128,2048]{1,2,0:T(8,128)(2,1)S(1)}, bf16[2,128,2048]{1,2,0:T(8,128)(2,1)S(1)}, u32[]{:S(2)}, u32[]{:S(2)}) collective-permute-start(bf16[2,128,2048]{1,2,0:T(8,128)(2,1)S(1)} %pad_maximum_fusion), channel_id=1, source_target_pairs={{0,2},{1,3},{2,4},{3,5},{4,6},{5,7},{6,8},{7,9},{8,10},{9,11},{10,... | collective-permute-start | bytes 3145736 | tf_op jit(solution)/shard_map/ppermute | solution.py:15
  760.8 147.1 %collective-permute-start.7 = (bf16[2,128,2048]{1,2,0:T(8,128)(2,1)S(1)}, bf16[2,128,2048]{1,2,0:T(8,128)(2,1)S(1)}, u32[]{:S(2)}, u32[]{:S(2)}) collective-permute-start(bf16[2,128,2048]{1,2,0:T(8,128)(2,1)S(1)} %pad_maximum_fusion), channel_id=1, source_target_pairs={{0,1},{1,2},{2,3},{3,4},{4,5},{5,6},{6,7},{7,8},{8,9},{9,10},{10,1... | collective-permute-start | bytes 3145736 | tf_op jit(solution)/shard_map/ppermute | solution.py:15
  911.8 3.7 copy-start
